TPU v7x, 32 devices: a whole 2x2x4 slice. The times are simulated.
32 devices in a mesh: space: 8 (over y, x, core), tm: 4 (over z).
Axes of the slice: x: 2, y: 2, z: 4, core: 2. Of those that a mesh axis runs over, the one named last changes fastest.
Arguments:
- series: bfloat16 [16384, 2, 512], P('space', None, 'tm'), may hold values from -6 to 6
- space_basis: bfloat16 [16384, 16384], P('space', 'tm'), may hold values from -0.046875 to 0.046875
- time_basis: bfloat16 [512, 512], P('tm'), may hold values from -0.25 to 0.25
- space_eig: float32 [16384], replicated, may hold values from 0.3 to 3
- time_eig: float32 [512], replicated, may hold values from 0.3 to 3
Outputs:
- alpha: bfloat16 [16384, 2, 512], P('space', None, 'tm')
- grad_space: bfloat16 [16384, 8, 2048], P('space', None, 'tm')
All inputs are finite; a program needn't handle non-finite values.
Results may differ from a plain program's by a relative error of at most 0.0063.
Values may be sent and summed in bfloat16 or wider, within the bound.
A program may use at most 128 MiB of HBM per device.

v0:
```python
import jax
import jax.numpy as jnp
from jax import lax
from jax.sharding import PartitionSpec as P

TIMES = 512
REPS = 2


def scale_block(spectral, eig_rows, eig_cols):
    denom = eig_rows[:, None] * eig_cols[None, :] + 0.1
    return (spectral / denom).astype(jnp.bfloat16)


def per_device(series, space_basis, time_basis, space_eig, time_eig):
    space_count = lax.axis_size("space")
    time_count = lax.axis_size("tm")
    time_idx = lax.axis_index("tm")
    row_count = space_basis.shape[0]
    col_block = space_basis.shape[1]
    time_local = time_basis.shape[0]
    wide_cols = REPS * TIMES
    sub_rows = row_count // time_count
    cols_tiled = jnp.tile(time_eig, REPS)
    full_series, full_basis = (
        lax.all_gather(series, "tm", axis=2, tiled=True),
        lax.all_gather(time_basis, "tm", axis=0, tiled=True),
    )
    rotated = jnp.dot(
        full_series.reshape(row_count * REPS, TIMES), full_basis, preferred_element_type=jnp.float32
    ).astype(jnp.bfloat16)
    rotated = rotated.reshape(row_count, wide_cols)
    contract_rows = (((0,), (0,)), ((), ()))
    partial_spec = lax.dot_general(
        space_basis, rotated, contract_rows, preferred_element_type=jnp.float32
    )
    spectral = lax.psum(partial_spec, "space")
    eig_rows = lax.dynamic_slice_in_dim(space_eig, time_idx * col_block, col_block)
    scaled_spec = scale_block(spectral, eig_rows, cols_tiled)
    back_part = jnp.dot(space_basis, scaled_spec, preferred_element_type=jnp.float32)
    back_all = lax.psum(back_part, "tm").astype(jnp.bfloat16)
    back_sub = lax.dynamic_slice_in_dim(back_all, time_idx * sub_rows, sub_rows, 0)
    contract_last = (((1,), (1,)), ((), ()))
    alpha = lax.dot_general(
        back_all.reshape(row_count * REPS, TIMES),
        time_basis,
        contract_last,
        preferred_element_type=jnp.float32,
    )
    alpha = alpha.astype(jnp.bfloat16).reshape(row_count, REPS, time_local)
    weighted = (
        back_all.reshape(row_count, REPS, TIMES).astype(jnp.float32) * time_eig[None, None, :]
    )
    weighted = (weighted / (REPS * TIMES)).astype(jnp.bfloat16).reshape(row_count, wide_cols)
    grad = lax.dot_general(
        weighted,
        lax.all_gather(back_sub, "space", axis=0, tiled=True),
        contract_last,
        preferred_element_type=jnp.float32,
    )
    grad = grad.astype(jnp.bfloat16).reshape(row_count, space_count, sub_rows)
    return (alpha, grad)


def solution(mesh):
    return jax.shard_map(
        per_device,
        mesh=mesh,
        in_specs=(P("space", None, "tm"), P("space", "tm"), P("tm", None), P(), P()),
        out_specs=(P("space", None, "tm"), P("space", None, "tm")),
        check_vma=False,
    )
```

profile of v0, /device:TPU:0, one launch (start us, length us, event | category | flops | bytes accessed | tf_op | source)
XLA Modules:
  0.0 778.3 jit_solution(7455162140651493963)
XLA Ops:
  7.2 0.0 copy-start
  7.2 0.0 all-gather.3.cloned.1.call-start
  7.2 0.7 all-gather.3.cloned.1.call-update
  7.9 0.0 all-reduce.3.cloned.1.call-start
  8.0 19.0 %all_gather.10 = bf16[512,512]{1,0:T(8,128)(2,1)S(1)} all-gather(bf16[128,512]{1,0:T(8,128)(2,1)} %param.7), channel_id=1, replica_groups=mesh['space'=8,'tm'=4] {'tm'}, dimensions={0}, use_global_device_ids=true | all-gather | bytes 655360 | tf_op jit(solution)/shard_map/all_gather | solution.py:27
  27.0 70.6 %all-gather.3.cloned.1.call-done = bf16[2048,2,512]{2,1,0:T(2,128)(2,1)} async-done(((bf16[2048,2,128]{2,1,0:T(2,128)(2,1)}), bf16[2048,2,512]{2,1,0:T(2,128)(2,1)}) %all-gather.3.cloned.1.call-update) | async-done | bytes 4194320 | tf_op jit(solution)/shard_map/all_gather | solution.py:26
  97.5 7.2 reshape.26
  104.7 6.5 convolution_convert_fusion.1
  111.2 7.1 reshape.27
  118.3 23.8 %convolution_bitcast_fusion = f32[4096,1024]{0,1:T(8,128)} fusion(bf16[2048,1024]{1,0:T(8,128)(2,1)} %reshape.27, bf16[2048,4096]{1,0:T(8,128)(2,1)} %param.6), kind=kOutput, calls=%fused_computation.2 | convolution fusion | flops 17179869184 | bytes 37748736 | tf_op jit(solution)/shard_map/dot_general | solution.py:34
  142.1 0.0 all-reduce.3.cloned.1.call-update
  142.2 0.0 all-gather.5.cloned.1.call-start
  142.2 0.0 copy-done
  142.2 0.7 dynamic_slice.6
  143.0 216.2 %all-reduce.3.cloned.1.call-done = f32[4096,1024]{0,1:T(8,128)} async-done(((f32[4096,1024]{0,1:T(8,128)}), f32[4096,1024]{0,1:T(8,128)}) %all-reduce.3.cloned.1.call-update) | async-done | bytes 16777232 | tf_op jit(solution)/shard_map/psum | solution.py:37
  359.2 26.6 %fusion.1 = f32[2048,1024]{0,1:T(8,128)} fusion(bf16[2048,4096]{1,0:T(8,128)(2,1)} %param.6, f32[4096,1024]{0,1:T(8,128)} %all-reduce.3.cloned.1.call-done, f32[1024]{0:T(1024)S(1)} %bitcast.21, f32[4096]{0:T(1024)S(1)} %dynamic_slice.6), kind=kOutput, calls=%fused_computation.7 | convolution fusion | flops 17196646400 | bytes 41963520 | tf_op jit(solution)/shard_map/dot_general | solution.py:40
  385.8 284.3 %all-reduce.4 = bf16[2048,1024]{0,1:T(8,128)(2,1)} all-reduce(f32[2048,1024]{0,1:T(8,128)} %fusion.1), channel_id=1, replica_groups=mesh['space'=8,'tm'=4] {'tm'}, use_global_device_ids=true, to_apply=%region_1.0 | all-reduce | flops 2097152 | bytes 12582912 | tf_op jit(solution)/shard_map/psum | solution.py:41
  670.1 2.3 constant_dynamic-slice_fusion
  672.4 0.0 all-gather.5.cloned.1.call-update
  672.4 0.0 copy-start.2
  672.4 6.4 copy.7
  678.9 7.2 reshape.28
  686.1 0.0 copy-done.2
  686.1 4.4 convolution_convert_fusion.2
  690.5 39.1 %all-gather.5.cloned.1.call-done = bf16[4096,1024]{0,1:T(8,128)(2,1)} async-done(((bf16[512,1024]{0,1:T(8,128)(2,1)}), bf16[4096,1024]{0,1:T(8,128)(2,1)}) %all-gather.5.cloned.1.call-update) | async-done | bytes 8388624 | tf_op jit(solution)/shard_map/all_gather | solution.py:57
  729.6 25.5 %convolution_convert_fusion = bf16[2048,4096]{1,0:T(8,128)(2,1)} fusion(bf16[4096,1024]{0,1:T(8,128)(2,1)} %all-gather.5.cloned.1.call-done, bf16[2048,1024]{0,1:T(8,128)(2,1)} %all-reduce.4, f32[1024]{0:T(1024)S(1)} %bitcast.22), kind=kOutput, calls=%fused_computation.1 | convolution fusion | flops 17196646400 | bytes 29364224 | tf_op jit(solution)/shard_map/dot_general | solution.py:55
  755.1 0.0 copy-start.1
  755.1 16.6 %copy.9 = bf16[256,8,8,512]{3,2,1,0:T(8,128)(2,1)} copy(bf16[256,8,8,512]{3,1,2,0:T(8,128)(2,1)} %bitcast.19) | data formatting | bytes 33554432
  771.8 0.0 copy-done.1
  (2 shorter events, 0.0 us)
Async XLA Ops:
  7.2 135.1 %copy-start = (f32[512]{0:T(512)S(1)}, f32[512]{0:T(512)}, u32[]{:S(2)}) copy-start(f32[512]{0:T(512)} %param.9) | copy-start | bytes 6148
  7.2 90.4 %all-gather.3.cloned.1.call-start = ((), (), s32[]{:S(2)}) async-start(), calls=%async_computation | async-start | bytes 5242880 | tf_op jit(solution)/shard_map/all_gather | solution.py:26
  7.9 351.3 %all-reduce.3.cloned.1.call-start = ((), (), s32[]{:S(2)}) async-start(), calls=%async_computation.1 | async-start | bytes 33554432 | tf_op jit(solution)/shard_map/psum | solution.py:37
  142.2 587.5 %all-gather.5.cloned.1.call-start = ((), (), s32[]{:S(2)}) async-start(), calls=%async_computation.2 | async-start | bytes 9437184 | tf_op jit(solution)/shard_map/all_gather | solution.py:57
  672.4 13.7 %copy-start.2 = (bf16[128,512]{1,0:T(8,128)(2,1)S(1)}, bf16[128,512]{1,0:T(8,128)(2,1)}, u32[]{:S(2)}) copy-start(bf16[128,512]{1,0:T(8,128)(2,1)} %param.7) | copy-start | bytes 393220
  755.1 16.6 %copy-start.1 = (f32[512]{0:T(512)S(1)}, f32[512]{0:T(512)}, u32[]{:S(2)}) copy-start(f32[512]{0:T(512)} %param.9) | copy-start | bytes 6148
Sparse Core Ops, SparseCore 0:
  9.5 87.9 all-gather.2
  142.3 216.8 all-reduce.2
  672.6 57.0 all-gather.4
where the time goes:
time: 779 us; the launch traced here: 778 us
  waiting for transfers between devices  327 us (42%)
  blocking collectives  303 us (39%)
  matrix products  86.8 us (11%)
  local copies, waits for them, and re-layouts  47.6 us (6%)
  between operations  13.8 us (2%)
    psum x1, blocking collectives, per_device(): back_all = lax.psum(back_part, 'tm').astype(jnp.bfloat16)  284 us
    psum x1, waiting for transfers between devices, per_device(): spectral = lax.psum(partial_spec, 'space')  216 us
    all_gather x1, waiting for transfers between devices, per_device(): lax.all_gather(series, 'tm', axis=2, tiled=True)  70.6 us
    all_gather x1, waiting for transfers between devices, per_device(): lax.all_gather(back_sub, 'space', axis=0, tiled=True)  39.1 us
    dot_general x1, matrix products, per_device(): jnp.dot(space_basis, scaled_spec, preferred_element_type=jnp.float32)  26.6 us
    dot_general x1, matrix products, per_device(): lax.dot_general(weighted, lax.all_gather(back_sub, 'space', axis=0, tiled...  25.5 us
    dot_general x1, matrix products, per_device(): lax.dot_general(space_basis, rotated, contract_rows, preferred_element_ty...  23.8 us
    all_gather x1, blocking collectives, per_device(): lax.all_gather(time_basis, 'tm', axis=0, tiled=True)  19 us
  transfers between devices with their start and end apart: 3, of which 3 were waited for; matrix products, arithmetic and copies ran while one was open for 2% of the time, Pallas kernels for 0%

commit v1 on v0

--- a/solution.py
+++ b/solution.py
@@ -38,7 +38,7 @@
     eig_rows = lax.dynamic_slice_in_dim(space_eig, time_idx * col_block, col_block)
     scaled_spec = scale_block(spectral, eig_rows, cols_tiled)
     back_part = jnp.dot(space_basis, scaled_spec, preferred_element_type=jnp.float32)
-    back_all = lax.psum(back_part, "tm").astype(jnp.bfloat16)
+    back_all = jnp.sum(lax.all_gather(back_part, "tm"), axis=0).astype(jnp.bfloat16)
     back_sub = lax.dynamic_slice_in_dim(back_all, time_idx * sub_rows, sub_rows, 0)
     contract_last = (((1,), (1,)), ((), ()))
     alpha = lax.dot_general(

time: 779 us -> 1120 us (1.44)
  waiting for transfers between devices: 327 us -> 885 us
  blocking collectives: 303 us -> 19 us
  local copies, waits for them, and re-layouts: 47.6 us -> 87.3 us
  other arithmetic: 0 us -> 25.4 us
    all_gather x0 -> x1, waiting for transfers between devices: none -> 561 us  [per_device(): lax.all_gather(back_part, 'tm')]
    psum x1 -> x0, blocking collectives: 284 us -> none  [per_device(): back_all = lax.psum(back_part, 'tm').astype(jnp.bfloat16)]
    all_gather x0 -> x1, local copies, waits for them, and re-layouts: none -> 39.6 us  [per_device(): lax.all_gather(back_part, 'tm')]
    reduce_sum x0 -> x1, other arithmetic: none -> 25.4 us  [per_device(): jnp.sum(lax.all_gather(back_part, 'tm'), axis=0).astype(jnp.bfloat16)]
  transfers between devices with their start and end apart: 3 -> 4, of which waited for: 3 -> 4; matrix products, arithmetic and copies ran while one was open for 2% -> 2% of each run, Pallas kernels for 0% -> 0%
where the time goes in v1:
time: 1120 us
  waiting for transfers between devices  885 us (79%)
  local copies, waits for them, and re-layouts  87.3 us (8%)
  matrix products  86.8 us (8%)
  other arithmetic  25.4 us (2%)
  blocking collectives  19 us (2%)
  between operations  13.8 us (1%)
    all_gather x1, waiting for transfers between devices, per_device(): lax.all_gather(back_part, 'tm')  561 us
    psum x1, waiting for transfers between devices, per_device(): spectral = lax.psum(partial_spec, 'space')  216 us
    all_gather x1, waiting for transfers between devices, per_device(): lax.all_gather(series, 'tm', axis=2, tiled=True)  70.6 us
    all_gather x1, local copies, waits for them, and re-layouts, per_device(): lax.all_gather(back_part, 'tm')  39.6 us
    all_gather x1, waiting for transfers between devices, per_device(): lax.all_gather(back_sub, 'space', axis=0, tiled=True)  36.1 us
    dot_general x1, matrix products, per_device(): jnp.dot(space_basis, scaled_spec, preferred_element_type=jnp.float32)  26.6 us
    dot_general x1, matrix products, per_device(): lax.dot_general(weighted, lax.all_gather(back_sub, 'space', axis=0, tiled...  25.5 us
    reduce_sum x1, other arithmetic, per_device(): jnp.sum(lax.all_gather(back_part, 'tm'), axis=0).astype(jnp.bfloat16)  25.4 us
  transfers between devices with their start and end apart: 4, of which 4 were waited for; matrix products, arithmetic and copies ran while one was open for 2% of the time, Pallas kernels for 0%

profile of v1, /device:TPU:0, one launch (start us, length us, event | category | flops | bytes accessed | tf_op | source)
XLA Modules:
  0.0 1117.6 jit_solution(6780517806397588570)
XLA Ops:
  7.2 0.0 copy-start
  7.2 0.0 all-gather.5.cloned.1.call-start
  7.2 0.7 all-gather.5.cloned.1.call-update
  7.9 0.0 all-reduce.2.cloned.1.call-start
  8.0 19.0 %all_gather.16 = bf16[512,512]{1,0:T(8,128)(2,1)S(1)} all-gather(bf16[128,512]{1,0:T(8,128)(2,1)} %param.7), channel_id=1, replica_groups=mesh['space'=8,'tm'=4] {'tm'}, dimensions={0}, use_global_device_ids=true | all-gather | bytes 655360 | tf_op jit(solution)/shard_map/all_gather | solution.py:27
  27.0 70.6 %all-gather.5.cloned.1.call-done = bf16[2048,2,512]{2,1,0:T(2,128)(2,1)} async-done(((bf16[2048,2,128]{2,1,0:T(2,128)(2,1)}), bf16[2048,2,512]{2,1,0:T(2,128)(2,1)}) %all-gather.5.cloned.1.call-update) | async-done | bytes 4194320 | tf_op jit(solution)/shard_map/all_gather | solution.py:26
  97.5 7.2 reshape.27
  104.7 6.5 convolution_convert_fusion.1
  111.2 7.1 reshape.28
  118.3 23.8 %convolution_bitcast_fusion = f32[4096,1024]{0,1:T(8,128)} fusion(bf16[2048,1024]{1,0:T(8,128)(2,1)} %reshape.28, bf16[2048,4096]{1,0:T(8,128)(2,1)} %param.6), kind=kOutput, calls=%fused_computation.2 | convolution fusion | flops 17179869184 | bytes 37748736 | tf_op jit(solution)/shard_map/dot_general | solution.py:34
  142.1 0.0 all-reduce.2.cloned.1.call-update
  142.2 0.0 all-gather.9.cloned.1.call-start
  142.2 0.0 copy-done
  142.3 0.7 dynamic_slice.6
  143.0 216.2 %all-reduce.2.cloned.1.call-done = f32[4096,1024]{0,1:T(8,128)} async-done(((f32[4096,1024]{0,1:T(8,128)}), f32[4096,1024]{0,1:T(8,128)}) %all-reduce.2.cloned.1.call-update) | async-done | bytes 16777232 | tf_op jit(solution)/shard_map/psum | solution.py:37
  359.2 26.6 %fusion.1 = f32[2048,1024]{0,1:T(8,128)} fusion(bf16[2048,4096]{1,0:T(8,128)(2,1)} %param.6, f32[4096,1024]{0,1:T(8,128)} %all-reduce.2.cloned.1.call-done, f32[1024]{0:T(1024)S(1)} %bitcast.23, f32[4096]{0:T(1024)S(1)} %dynamic_slice.6), kind=kOutput, calls=%fused_computation.7 | convolution fusion | flops 17196646400 | bytes 41963520 | tf_op jit(solution)/shard_map/dot_general | solution.py:40
  385.8 0.0 all-gather.9.cloned.1.call-update
  385.9 0.2 all-gather.7.cloned.1.call-start
  386.1 561.3 %all-gather.9.cloned.1.call-done = f32[8192,1024]{0,1:T(8,128)} async-done(((f32[2048,1024]{0,1:T(8,128)}), f32[8192,1024]{0,1:T(8,128)}) %all-gather.9.cloned.1.call-update) | async-done | bytes 33554448 | tf_op jit(solution)/shard_map/all_gather | solution.py:41
  947.4 39.6 %reshape.31 = f32[4,2048,1024]{1,0,2:T(4,128)} reshape(f32[8192,1024]{0,1:T(8,128)} %all-gather.9.cloned.1.call-done) | data formatting | bytes 67108864 | tf_op jit(solution)/shard_map/all_gather | solution.py:41
  987.0 25.4 %reduce_sum.9 = bf16[2048,1024]{0,1:T(8,128)(2,1)} reduce(f32[4,2048,1024]{1,0,2:T(4,128)} %reshape.31, f32[]{:T(128)} %constant.6.clone.1), dimensions={0}, to_apply=%region_1.0 | reduce | flops 6291456 | bytes 37748740 | tf_op jit(solution)/shard_map/reduce_sum | solution.py:41
  1012.3 2.3 constant_dynamic-slice_fusion
  1014.7 0.0 all-gather.7.cloned.1.call-update
  1014.7 0.0 copy-start.2
  1014.7 6.5 copy.7
  1021.2 7.2 convert_element_type.32
  1028.4 0.0 copy-done.2
  1028.4 4.4 convolution_convert_fusion.2
  1032.8 36.1 %all-gather.7.cloned.1.call-done = bf16[4096,1024]{0,1:T(8,128)(2,1)} async-done(((bf16[512,1024]{0,1:T(8,128)(2,1)}), bf16[4096,1024]{0,1:T(8,128)(2,1)}) %all-gather.7.cloned.1.call-update) | async-done | bytes 8388624 | tf_op jit(solution)/shard_map/all_gather | solution.py:57
  1068.9 25.5 %convolution_convert_fusion = bf16[2048,4096]{1,0:T(8,128)(2,1)} fusion(bf16[4096,1024]{0,1:T(8,128)(2,1)} %all-gather.7.cloned.1.call-done, bf16[2048,1024]{0,1:T(8,128)(2,1)} %reduce_sum.9, f32[1024]{0:T(1024)S(1)} %bitcast.24), kind=kOutput, calls=%fused_computation.1 | convolution fusion | flops 17196646400 | bytes 29364224 | tf_op jit(solution)/shard_map/dot_general | solution.py:55
  1094.4 0.0 copy-start.1
  1094.4 16.6 %copy.9 = bf16[256,8,8,512]{3,2,1,0:T(8,128)(2,1)} copy(bf16[256,8,8,512]{3,1,2,0:T(8,128)(2,1)} %bitcast.21) | data formatting | bytes 33554432
  1111.1 0.0 copy-done.1
  (2 shorter events, 0.0 us)
Async XLA Ops:
  7.2 135.1 %copy-start = (f32[512]{0:T(512)S(1)}, f32[512]{0:T(512)}, u32[]{:S(2)}) copy-start(f32[512]{0:T(512)} %param.9) | copy-start | bytes 6148
  7.2 90.4 %all-gather.5.cloned.1.call-start = ((), (), s32[]{:S(2)}) async-start(), calls=%async_computation | async-start | bytes 5242880 | tf_op jit(solution)/shard_map/all_gather | solution.py:26
  7.9 351.3 %all-reduce.2.cloned.1.call-start = ((), (), s32[]{:S(2)}) async-start(), calls=%async_computation.1 | async-start | bytes 33554432 | tf_op jit(solution)/shard_map/psum | solution.py:37
  142.2 805.2 %all-gather.9.cloned.1.call-start = ((), (), s32[]{:S(2)}) async-start(), calls=%async_computation.3 | async-start | bytes 41943040 | tf_op jit(solution)/shard_map/all_gather | solution.py:41
  385.9 683.0 %all-gather.7.cloned.1.call-start = ((), (), s32[]{:S(2)}) async-start(), calls=%async_computation.2 | async-start | bytes 9437184 | tf_op jit(solution)/shard_map/all_gather | solution.py:57
  1014.7 13.7 %copy-start.2 = (bf16[128,512]{1,0:T(8,128)(2,1)S(1)}, bf16[128,512]{1,0:T(8,128)(2,1)}, u32[]{:S(2)}) copy-start(bf16[128,512]{1,0:T(8,128)(2,1)} %param.7) | copy-start | bytes 393220
  1094.4 16.6 %copy-start.1 = (f32[512]{0:T(512)S(1)}, f32[512]{0:T(512)}, u32[]{:S(2)}) copy-start(f32[512]{0:T(512)} %param.9) | copy-start | bytes 6148
Sparse Core Ops, SparseCore 0:
  9.5 87.9 all-gather.4
  142.3 216.8 all-reduce.1
  386.0 561.3 all-gather.8
  1014.8 54.0 all-gather.6
